TPU v7x, 32 devices: a whole 2x2x4 slice. The times are simulated.
32 devices in a mesh: groups: 2 (over y), seq: 4 (over z), head: 2 (over x), rep: 2 (over core).
Axes of the slice: x: 2, y: 2, z: 4, core: 2. Of those that a mesh axis runs over, the one named last changes fastest.
Arguments:
- tokens: bfloat16 [4096, 5376], P(('groups', 'seq'), ('head', 'rep')), parts along dimension 0, may hold values from -6 to 6
- query_matrix: bfloat16 [5376, 2048], P(None, ('head', 'rep')), may hold values from -0.078125 to 0.078125
- key_matrix: bfloat16 [5376, 1024], P(None, 'head'), may hold values from -0.078125 to 0.078125
- value_matrix: bfloat16 [5376, 1024], P(None, 'head'), may hold values from -0.078125 to 0.078125
- output_matrix: bfloat16 [2048, 5376], P(None, ('head', 'rep')), may hold values from -0.125 to 0.125
- query_gain: float32 [128], replicated, may hold values from 0.1 to 1.9
- key_norm_gain: float32 [128], replicated, may hold values from 0.1 to 1.9
- adapter_down: bfloat16 [8, 5376, 96], P('seq', ('head', 'rep')), may hold values from -0.078125 to 0.078125
- adapter_up_query: bfloat16 [8, 32, 2048], P('seq', None, ('head', 'rep')), may hold values from -1 to 1
- key_value_up_panels: bfloat16 [8, 2, 32, 1024], P('seq', None, None, 'head'), may hold values from -1 to 1
- adapter_out_down: bfloat16 [8, 2048, 32], P('seq', ('head', 'rep')), may hold values from -0.125 to 0.125
- adapter_out_up: bfloat16 [8, 32, 5376], P('seq', None, ('head', 'rep')), may hold values from -1 to 1
- request_of_block: int32 [32], P('groups'), parts along dimension 0, may hold values from 0 to 1, never falling along the last dimension, each value on 1 to 12 neighbouring positions
- adapter_of_request: int32 [4], P('groups'), parts along dimension 0, may hold values from 0 to 7
Outputs:
- result: bfloat16 [4096, 5376], P(('groups', 'seq'), ('head', 'rep')), parts along dimension 0
There are 2 independent parts, one for each index of `groups`. A program takes and returns all parts, laid end to end along the dimension named above; an argument that names none is the same for every part. Nothing has to cross between parts.
Inputs may be any that keep to these rules, and one draw needn't show every extreme that they name: `request_of_block`: never falls from one block to the next; every request has 1 to 12 blocks.
All inputs are finite; a program needn't handle non-finite values.
Results may differ from a plain program's by a relative error of at most 0.014.
Values may be sent and summed in bfloat16 or wider, within the bound.
No kernel may reach another device: no remote copies, remote signals or barrier semaphores. Data moves between devices by JAX's collectives and lax.ppermute only.
A program may use at most 128 MiB of HBM per device.

v0:
```python
import math
import jax
import jax.numpy as jnp
from jax import lax
from jax.sharding import PartitionSpec as P

HEAD_SIZE = 128
ADAPTER_RANK = 32
KEY_WINDOW = 1024
BLOCK = 128
norm_epsilon = 1e-06
rope_base = 10000.0
score_scale = 168.0 ** (-0.5)
adapter_scale = 2.0


def shifted(value, axis, by):
    size = lax.axis_size(axis)
    pairs = [(i, i + by) for i in range(size) if 0 <= i + by < size]
    return lax.ppermute(value, axis, pairs)


def per_head_norm(values, scale_gain):
    mean_square = jnp.mean(values * values, axis=-1, keepdims=True)
    return values * lax.rsqrt(mean_square + norm_epsilon) * scale_gain


def rope_tables(positions, head_dim):
    half_dim = head_dim // 2
    frequency = jnp.power(rope_base, -jnp.arange(half_dim, dtype=jnp.float32) * 2.0 / head_dim)
    angles = positions.astype(jnp.float32)[:, None] * frequency[None, :]
    return (jnp.cos(angles), jnp.sin(angles))


def rotate_feature_pairs(values, cosine_table, sine_values):
    half_dim = values.shape[-1] // 2
    first_half = values[..., :half_dim]
    second_half = values[..., half_dim:]
    cosine_table = cosine_table[:, None, :]
    sine_values = sine_values[:, None, :]
    return jnp.concatenate(
        [
            first_half * cosine_table - second_half * sine_values,
            second_half * cosine_table + first_half * sine_values,
        ],
        axis=-1,
    )


def request_starts(block_requests, all_requests):
    earlier = (all_requests[None, :] < block_requests[:, None]).astype(jnp.int32)
    return jnp.sum(earlier, axis=1) * BLOCK


def per_device(
    tokens,
    query_matrix,
    key_matrix,
    value_matrix,
    output_matrix,
    query_gain,
    key_norm_gain,
    adapter_down,
    adapter_up_query,
    key_value_up_panels,
    adapter_out_down,
    adapter_out_up,
    request_of_block,
    adapter_of_request,
):
    tok_rows, width_part = tokens.shape
    query_cols = query_matrix.shape[1]
    key_cols = key_matrix.shape[1]
    query_heads = query_cols // HEAD_SIZE
    block_count = tok_rows // BLOCK
    all_blocks = request_of_block.shape[0]
    request_total = adapter_of_request.shape[0]
    seq_index = lax.axis_index("seq")
    rep_index = lax.axis_index("rep")
    first_row = seq_index * tok_rows
    own_requests = lax.dynamic_slice_in_dim(
        request_of_block, seq_index * block_count, block_count, 0
    )
    request_match = own_requests[:, None] == jnp.arange(request_total, dtype=jnp.int32)[None, :]
    own_adapters = jnp.sum(jnp.where(request_match, adapter_of_request[None, :], 0), axis=1)
    pool_part = (
        lax.all_gather(adapter_down, "seq", axis=0, tiled=True),
        lax.all_gather(adapter_up_query, "seq", axis=0, tiled=True),
        lax.all_gather(key_value_up_panels, "seq", axis=0, tiled=True),
        lax.all_gather(adapter_out_down, "seq", axis=0, tiled=True),
        lax.all_gather(adapter_out_up, "seq", axis=0, tiled=True),
    )
    held_count = pool_part[0].shape[0]
    select = (own_adapters[:, None] == jnp.arange(held_count, dtype=jnp.int32)[None, :]).astype(
        jnp.bfloat16
    )
    (
        picked_down_panels,
        picked_query_panels,
        picked_key_panels,
        chosen_out_down,
        picked_output_up,
    ) = tuple(
        (
            jnp.einsum(
                "bn,n...->b...", select, panel_part, preferred_element_type=jnp.float32
            ).astype(jnp.bfloat16)
            for panel_part in pool_part
        )
    )
    token_block_list = tokens.reshape(block_count, BLOCK, width_part)
    partial_low = jnp.einsum(
        "myj,mjc->myc", token_block_list, picked_down_panels, preferred_element_type=jnp.float32
    ).reshape(tok_rows, 3 * ADAPTER_RANK)
    reduced_rank_rows = (
        lax.psum(partial_low, ("head", "rep"))
        .astype(jnp.bfloat16)
        .reshape(block_count, BLOCK, 3 * ADAPTER_RANK)
    )
    feature_part = lax.all_gather(tokens, ("head", "rep"), axis=1, tiled=True)
    query_add = jnp.dot(feature_part, query_matrix, preferred_element_type=jnp.float32)
    key_add = jnp.dot(feature_part, key_matrix, preferred_element_type=jnp.float32)
    value_add = jnp.dot(feature_part, value_matrix, preferred_element_type=jnp.float32)
    query_linear = query_add
    key_linear = key_add
    value_linear = value_add
    query_linear = query_linear + adapter_scale * jnp.einsum(
        "tlq,tqo->tlo",
        reduced_rank_rows[..., :ADAPTER_RANK],
        picked_query_panels,
        preferred_element_type=jnp.float32,
    ).reshape(tok_rows, query_cols)
    key_linear = key_linear + adapter_scale * jnp.einsum(
        "tlq,tqo->tlo",
        reduced_rank_rows[..., ADAPTER_RANK : 2 * ADAPTER_RANK],
        picked_key_panels[:, 0],
        preferred_element_type=jnp.float32,
    ).reshape(tok_rows, key_cols)
    value_linear = value_linear + adapter_scale * jnp.einsum(
        "tlq,tqo->tlo",
        reduced_rank_rows[..., 2 * ADAPTER_RANK :],
        picked_key_panels[:, 1],
        preferred_element_type=jnp.float32,
    ).reshape(tok_rows, key_cols)
    key_full = key_linear.astype(jnp.bfloat16)
    value_full = value_linear.astype(jnp.bfloat16)
    key_heads = key_cols // HEAD_SIZE
    token_index = first_row + jnp.arange(tok_rows, dtype=jnp.int32)
    token_request = jnp.repeat(own_requests, BLOCK)
    token_start = jnp.repeat(request_starts(own_requests, request_of_block), BLOCK)
    cosine_table, sine_values = rope_tables(token_index - token_start, HEAD_SIZE)
    query_rows = (
        rotate_feature_pairs(
            per_head_norm(query_linear.reshape(tok_rows, query_heads, HEAD_SIZE), query_gain),
            cosine_table,
            sine_values,
        )
        * score_scale
    ).astype(jnp.bfloat16)
    rotated_keys = rotate_feature_pairs(
        per_head_norm(
            key_full.astype(jnp.float32).reshape(tok_rows, key_heads, HEAD_SIZE), key_norm_gain
        ),
        cosine_table,
        sine_values,
    ).astype(jnp.bfloat16)
    group_heads = max(query_heads // 2, 1)
    group_size = query_heads // group_heads
    head_first = rep_index * query_heads // 2
    keys_used = lax.dynamic_slice_in_dim(rotated_keys, head_first, group_heads, 1).reshape(
        tok_rows, group_heads * HEAD_SIZE
    )
    values_used = lax.dynamic_slice_in_dim(
        value_full.reshape(tok_rows, key_heads, HEAD_SIZE), head_first, group_heads, 1
    ).reshape(tok_rows, group_heads * HEAD_SIZE)
    query_groups = query_rows.reshape(tok_rows, group_heads, group_size, HEAD_SIZE)
    block_table = jnp.arange(all_blocks, dtype=jnp.int32)
    empty_state = (
        jnp.zeros((tok_rows, group_heads, group_size, HEAD_SIZE), jnp.float32),
        jnp.zeros((group_heads, group_size, tok_rows), jnp.float32),
    )
    reach_blocks = KEY_WINDOW // tok_rows
    stacked = jnp.stack((keys_used, values_used))
    earlier = []
    for step_back in range(reach_blocks, 0, -1):
        earlier.append(shifted(stacked, "seq", step_back))
    window_stack = jnp.concatenate(earlier + [stacked], axis=1)
    fold_state = empty_state
    offset = first_row - reach_blocks * tok_rows
    key_block = window_stack[0]
    value_block = window_stack[1]
    key_length = key_block.shape[0]
    step_length = math.gcd(key_length, 512)
    steps_count = key_length // step_length
    key_steps = key_block.reshape(steps_count, step_length, group_heads, HEAD_SIZE)
    value_steps = value_block.reshape(steps_count, step_length, group_heads, HEAD_SIZE)

    def one_step(carry_state, step_inputs):
        step_keys, step_values, step_index = step_inputs
        key_position = offset + step_index * step_length + jnp.arange(step_length, dtype=jnp.int32)
        key_block_id = jnp.clip(key_position, 0, all_blocks * BLOCK - 1) // BLOCK
        key_request = jnp.sum(
            jnp.where(key_block_id[:, None] == block_table[None, :], request_of_block[None, :], 0),
            axis=1,
        )
        distance = token_index[:, None] - key_position[None, :]
        allowed = (
            (key_position[None, :] >= 0)
            & (distance >= 0)
            & (distance < KEY_WINDOW)
            & (token_request[:, None] == key_request[None, :])
        )
        scores = jnp.einsum(
            "tcpd,kcd->cptk", query_groups, step_keys, preferred_element_type=jnp.float32
        )
        weights = jnp.where(allowed[None, None], jnp.exp(scores), 0.0)
        numerator, denominator = carry_state
        denominator = denominator + jnp.sum(weights, axis=-1)
        numerator = numerator + jnp.einsum(
            "cptk,kcd->tcpd",
            weights.astype(jnp.bfloat16),
            step_values,
            preferred_element_type=jnp.float32,
        )
        return ((numerator, denominator), None)

    fold_state, unused_out = lax.scan(
        one_step, fold_state, (key_steps, value_steps, jnp.arange(steps_count, dtype=jnp.int32))
    )
    numerator, denominator = fold_state
    attention_result = (
        (numerator / jnp.transpose(denominator, (2, 0, 1))[..., None])
        .astype(jnp.bfloat16)
        .reshape(tok_rows, query_cols)
    )
    output_zero = (
        jnp.zeros((tok_rows, width_part), jnp.float32),
        jnp.zeros((tok_rows, ADAPTER_RANK), jnp.float32),
    )
    projected_rows = jnp.dot(
        lax.all_gather(attention_result, ("head", "rep"), axis=1, tiled=True),
        output_matrix,
        preferred_element_type=jnp.float32,
    )
    projected_rows, lowered = (projected_rows, output_zero[1])
    local_low = jnp.einsum(
        "bkc,bcr->bkr",
        attention_result.reshape(block_count, BLOCK, query_cols),
        chosen_out_down,
        preferred_element_type=jnp.float32,
    ).reshape(tok_rows, ADAPTER_RANK)
    output_reduced_rank = lax.psum(local_low, ("head", "rep")).astype(jnp.bfloat16)
    result = projected_rows + adapter_scale * jnp.einsum(
        "zch,zhp->zcp",
        output_reduced_rank.reshape(block_count, BLOCK, ADAPTER_RANK),
        picked_output_up,
        preferred_element_type=jnp.float32,
    ).reshape(tok_rows, width_part)
    return result.astype(jnp.bfloat16)


def solution(mesh):
    return jax.shard_map(
        per_device,
        mesh=mesh,
        in_specs=(
            P(("groups", "seq"), ("head", "rep")),
            P(None, ("head", "rep")),
            P(None, "head"),
            P(None, "head"),
            P(None, ("head", "rep")),
            P(),
            P(),
            P("seq", ("head", "rep"), None),
            P("seq", None, ("head", "rep")),
            P("seq", None, None, "head"),
            P("seq", ("head", "rep"), None),
            P("seq", None, ("head", "rep")),
            P("groups"),
            P("groups"),
        ),
        out_specs=P(("groups", "seq"), ("head", "rep")),
        check_vma=False,
    )
```

profile of v0, /device:TPU:0, one launch (start us, length us, event | category | flops | bytes accessed | tf_op | source)
XLA Modules:
  0.0 259.6 jit_solution(15790281969873115158)
XLA Ops:
  6.5 0.7 all-gather.6.cloned.1.call-update
  7.3 0.7 all-gather.4.cloned.1.call-update
  8.1 0.8 dynamic_slice.29
  8.9 16.8 %all_gather.24 = bf16[8,32,512]{2,1,0:T(8,128)(2,1)S(1)} all-gather(bf16[2,32,512]{2,1,0:T(8,128)(2,1)} %param.24), channel_id=1, replica_groups=mesh['groups'=2,'seq'=4,'head'=2,'rep'=2] {'seq'}, dimensions={0}, use_global_device_ids=true | all-gather | bytes 327680 | tf_op jit(solution)/shard_map/all_gather | solution.py:88
  25.8 0.8 convert_reduce_fusion
  26.6 0.7 fusion.62
  27.3 23.4 %all_gather.23 = bf16[8,2,32,512]{3,2,1,0:T(8,128)(2,1)S(1)} all-gather(bf16[2,2,32,512]{3,2,1,0:T(8,128)(2,1)} %param.25), channel_id=1, replica_groups=mesh['groups'=2,'seq'=4,'head'=2,'rep'=2] {'seq'}, dimensions={0}, use_global_device_ids=true | all-gather | bytes 655360 | tf_op jit(solution)/shard_map/all_gather | solution.py:89
  50.9 0.5 multiply_cosine_fusion
  51.4 0.4 convolution_convert_fusion.2
  52.2 15.6 %all-gather.6.cloned.1.call-done = bf16[8,1344,96]{1,2,0:T(8,128)(2,1)} async-done(((bf16[2,1344,96]{1,2,0:T(8,128)(2,1)}), bf16[8,1344,96]{1,2,0:T(8,128)(2,1)}) %all-gather.6.cloned.1.call-update) | async-done | bytes 2064400 | tf_op jit(solution)/shard_map/all_gather | solution.py:87
  67.8 2.6 convolution_convert_fusion
  70.4 0.5 fusion.35
  70.9 16.8 %all-reduce.1 = bf16[512,96]{0,1:T(8,128)(2,1)S(1)} all-reduce(f32[512,96]{0,1:T(8,128)S(1)} %bitcast.140), channel_id=1, replica_groups=mesh['groups'=2,'seq'=4,'head'=2,'rep'=2] {'head','rep'}, use_global_device_ids=true, to_apply=%region_1.2 | all-reduce | flops 49152 | bytes 294912 | tf_op jit(solution)/shard_map/psum | solution.py:116
  88.2 1.3 copy.113
  90.8 21.5 %all-gather.4.cloned.1.call-done = bf16[512,5376]{0,1:T(8,128)(2,1)} async-done(((bf16[512,1344]{0,1:T(8,128)(2,1)}), bf16[512,5376]{0,1:T(8,128)(2,1)}) %all-gather.4.cloned.1.call-update) | async-done | bytes 5505040 | tf_op jit(solution)/shard_map/all_gather | solution.py:120
  112.4 7.6 %fusion.39 = (f32[512,4]{0,1:T(4,128)S(1)}, bf16[512,512]{0,1:T(8,128)(2,1)S(1)}) fusion(f32[512,512]{0,1:T(8,128)} %copy.113, bf16[512,5376]{0,1:T(8,128)(2,1)} %all-gather.4.cloned.1.call-done, bf16[5376,512]{1,0:T(8,128)(2,1)} %param.18), kind=kOutput, calls=%fused_computation.63 | convolution fusion | flops 2819880960 | bytes 12591104 | tf_op jit(solution)/shard_map/dot_general | solution.py:122
  120.1 5.2 %multiply_reduce_fusion = (f32[512,4]{0,1:T(4,128)S(1)}, f32[512,512]{0,1:T(8,128)S(1)}) fusion(f32[512,512]{0,1:T(8,128)S(1)} %copy.96, bf16[512,5376]{0,1:T(8,128)(2,1)S(1)} %copy-done.7, bf16[5376,512]{1,0:T(8,128)(2,1)} %param.17), kind=kOutput, calls=%fused_computation.69 | convolution fusion | flops 2819356672 | bytes 13115392 | tf_op jit(solution)/shard_map/dot_general | solution.py:121
  125.7 1.1 multiply_subtract_fusion
  126.8 3.0 %fusion.34 = bf16[512,512]{0,1:T(8,128)(2,1)S(1)} fusion(f32[512,512]{0,1:T(8,128)S(1)} %copy.91, bf16[512,5376]{0,1:T(8,128)(2,1)S(1)} %copy-done.7, bf16[5376,512]{1,0:T(8,128)(2,1)S(1)} %bitcast.145), kind=kOutput, calls=%fused_computation.56 | convolution fusion | flops 2819096576 | bytes 12582912 | tf_op jit(solution)/shard_map/dot_general | solution.py:123
  130.2 0.9 pad_maximum_fusion
  131.1 4.3 %collective-permute-start = (bf16[2,512,256]{2,1,0:T(8,128)(2,1)}, bf16[2,512,256]{2,1,0:T(8,128)(2,1)}, u32[]{:S(2)}, u32[]{:S(2)}) collective-permute-start(bf16[2,512,256]{2,1,0:T(8,128)(2,1)} %pad_maximum_fusion), channel_id=1, source_target_pairs={{0,8},{4,12},{1,9},{5,13},{2,10},{6,14},{3,11},{7,15},{16,24},{20,... | collective-permute-start | bytes 1572872 | tf_op jit(solution)/shard_map/ppermute | solution.py:20
  135.5 3.9 %collective-permute-start.1 = (bf16[2,512,256]{2,1,0:T(8,128)(2,1)}, bf16[2,512,256]{2,1,0:T(8,128)(2,1)}, u32[]{:S(2)}, u32[]{:S(2)}) collective-permute-start(bf16[2,512,256]{2,1,0:T(8,128)(2,1)} %pad_maximum_fusion), channel_id=1, source_target_pairs={{0,4},{4,8},{8,12},{1,5},{5,9},{9,13},{2,6},{6,10},{10,14},{3,7},{... | collective-permute-start | bytes 1572872 | tf_op jit(solution)/shard_map/ppermute | solution.py:20
  139.7 1.4 copy.98
  141.1 1.1 fusion.41
  142.3 5.1 %collective-permute-done = bf16[2,512,256]{2,1,0:T(8,128)(2,1)} collective-permute-done((bf16[2,512,256]{2,1,0:T(8,128)(2,1)}, bf16[2,512,256]{2,1,0:T(8,128)(2,1)}, u32[]{:S(2)}, u32[]{:S(2)}) %collective-permute-start) | collective-permute-done | bytes 524320 | tf_op jit(solution)/shard_map/ppermute | solution.py:20
  147.3 10.6 %collective-permute-done.1 = bf16[2,512,256]{2,1,0:T(8,128)(2,1)} collective-permute-done((bf16[2,512,256]{2,1,0:T(8,128)(2,1)}, bf16[2,512,256]{2,1,0:T(8,128)(2,1)}, u32[]{:S(2)}, u32[]{:S(2)}) %collective-permute-start.1) | collective-permute-done | bytes 524320 | tf_op jit(solution)/shard_map/ppermute | solution.py:20
  157.9 1.4 maximum_maximum_fusion
  159.9 29.6 %while.15 = (s32[]{:T(128)}, f32[512,2,2,128]{0,3,2,1:T(8,128)S(1)}, f32[2,2,512]{2,1,0:T(2,128)S(1)}, bf16[3,512,2,128]{3,2,1,0:T(2,128)(2,1)S(1)}, s32[3]{0:T(...) while((s32[]{:T(128)}, ...), condition=%wide.region_8.9_spmd.clone, body=%wide.region_5.8_spmd.clone.sunk | while | flops 543460864 | bytes 13948180 | solution.py:227
  159.9 0.6 dynamic_slice.49
  161.4 0.5 fusion.92
  161.9 0.4 constant_dynamic-slice_fusion.4
  162.3 4.0 %fusion.93 = (f32[2,2,512]{2,1,0:T(2,128)S(1)}, f32[2,512,512,2]{2,1,3,0:T(8,128)}) fusion(pred[512,512]{0,1:T(8,128)(4,1)S(1)} %fusion.92, bf16[512,2,2,128]{3,0,2,1:T(8,128)(2,1)} %get-tuple-element.399, bf16[1,512,2,128]{3,2,1,0:T(2,128)(2,1)S(1)} %get-tuple-element.359), kind=kOutput, calls=%fused_computation.4.clone.1 | convolution fusion | flops 270530560 | bytes 5251072 | tf_op jit(solution)/shard_map/while/body/eval_jaxpr/tcpd,kcd->cptk/dot_general | solution.py:213
  166.5 3.2 %fusion.94 = f32[512,2,2,128]{0,3,2,1:T(8,128)S(1)} fusion(f32[2,512,512,2]{2,1,3,0:T(8,128)} %get-tuple-element.360, pred[512,512]{0,1:T(8,128)(4,1)S(1)} %fusion.92, f32[512,2,2,128]{0,3,2,1:T(8,128)S(1)} %get-tuple-element.378, pred[]{:T(512)S(6)} %compare.16, bf16[1,512,2,128]{1,3,2,0:T(8,128)(2,1)S(1)} %copy.178), kind=kOutput, calls=%fused_computation.12.clone.1 | convolution fusion | flops 271056896 | bytes 6815745 | tf_op jit(solution)/shard_map/while/body/eval_jaxpr/cptk,kcd->tcpd/dot_general | solution.py:219
  169.8 0.7 dynamic_slice.49
  171.3 0.5 fusion.92
  172.1 4.1 %fusion.93 = (f32[2,2,512]{2,1,0:T(2,128)S(1)}, f32[2,512,512,2]{2,1,3,0:T(8,128)}) fusion(pred[512,512]{0,1:T(8,128)(4,1)S(1)} %fusion.92, bf16[512,2,2,128]{3,0,2,1:T(8,128)(2,1)} %get-tuple-element.399, bf16[1,512,2,128]{3,2,1,0:T(2,128)(2,1)S(1)} %get-tuple-element.359), kind=kOutput, calls=%fused_computation.4.clone.1 | convolution fusion | flops 270530560 | bytes 5251072 | tf_op jit(solution)/shard_map/while/body/eval_jaxpr/tcpd,kcd->cptk/dot_general | solution.py:213
  176.4 3.2 %fusion.94 = f32[512,2,2,128]{0,3,2,1:T(8,128)S(1)} fusion(f32[2,512,512,2]{2,1,3,0:T(8,128)} %get-tuple-element.360, pred[512,512]{0,1:T(8,128)(4,1)S(1)} %fusion.92, f32[512,2,2,128]{0,3,2,1:T(8,128)S(1)} %get-tuple-element.378, pred[]{:T(512)S(6)} %compare.16, bf16[1,512,2,128]{1,3,2,0:T(8,128)(2,1)S(1)} %copy.178), kind=kOutput, calls=%fused_computation.12.clone.1 | convolution fusion | flops 271056896 | bytes 6815745 | tf_op jit(solution)/shard_map/while/body/eval_jaxpr/cptk,kcd->tcpd/dot_general | solution.py:219
  179.7 0.7 dynamic_slice.49
  181.2 0.5 fusion.92
  182.0 4.1 %fusion.93 = (f32[2,2,512]{2,1,0:T(2,128)S(1)}, f32[2,512,512,2]{2,1,3,0:T(8,128)}) fusion(pred[512,512]{0,1:T(8,128)(4,1)S(1)} %fusion.92, bf16[512,2,2,128]{3,0,2,1:T(8,128)(2,1)} %get-tuple-element.399, bf16[1,512,2,128]{3,2,1,0:T(2,128)(2,1)S(1)} %get-tuple-element.359), kind=kOutput, calls=%fused_computation.4.clone.1 | convolution fusion | flops 270530560 | bytes 5251072 | tf_op jit(solution)/shard_map/while/body/eval_jaxpr/tcpd,kcd->cptk/dot_general | solution.py:213
  186.3 3.2 %fusion.94 = f32[512,2,2,128]{0,3,2,1:T(8,128)S(1)} fusion(f32[2,512,512,2]{2,1,3,0:T(8,128)} %get-tuple-element.360, pred[512,512]{0,1:T(8,128)(4,1)S(1)} %fusion.92, f32[512,2,2,128]{0,3,2,1:T(8,128)S(1)} %get-tuple-element.378, pred[]{:T(512)S(6)} %compare.16, bf16[1,512,2,128]{1,3,2,0:T(8,128)(2,1)S(1)} %copy.178), kind=kOutput, calls=%fused_computation.12.clone.1 | convolution fusion | flops 271056896 | bytes 6815745 | tf_op jit(solution)/shard_map/while/body/eval_jaxpr/cptk,kcd->tcpd/dot_general | solution.py:219
  189.6 0.9 divide_convert_fusion
  190.5 26.5 %all_gather.26 = bf16[8,512,32]{1,2,0:T(8,128)(2,1)S(1)} all-gather(bf16[2,512,32]{1,2,0:T(8,128)(2,1)S(1)} %copy-done.3), channel_id=1, replica_groups=mesh['groups'=2,'seq'=4,'head'=2,'rep'=2] {'seq'}, dimensions={0}, use_global_device_ids=true | all-gather | bytes 327680 | tf_op jit(solution)/shard_map/all_gather | solution.py:90
  217.3 16.2 %all_gather.27 = bf16[8,32,1344]{2,1,0:T(8,128)(2,1)S(1)} all-gather(bf16[2,32,1344]{2,1,0:T(8,128)(2,1)} %param.27), channel_id=1, replica_groups=mesh['groups'=2,'seq'=4,'head'=2,'rep'=2] {'seq'}, dimensions={0}, use_global_device_ids=true | all-gather | bytes 860160 | tf_op jit(solution)/shard_map/all_gather | solution.py:91
  233.5 0.4 convolution_convert_fusion.1
  234.3 10.7 %psum.15 = bf16[512,32]{0,1:T(8,128)(2,1)S(1)} all-reduce(f32[512,32]{0,1:T(8,128)S(1)} %bitcast.142), channel_id=1, replica_groups=mesh['groups'=2,'seq'=4,'head'=2,'rep'=2] {'head','rep'}, use_global_device_ids=true, to_apply=%region_9.10 | all-reduce | flops 16384 | bytes 98304 | tf_op jit(solution)/shard_map/psum | solution.py:252
  245.0 0.7 fusion.29
  245.7 7.3 %fusion.27 = bf16[512,1344]{0,1:T(8,128)(2,1)} fusion(bf16[2048,1344]{0,1:T(8,128)(2,1)} %param.20, bf16[512,2048]{0,1:T(8,128)(2,1)} %all-gather.8.cloned.1.call-done, f32[4,168,8,128]{3,2,1,0:T(8,128)S(1)} %fusion.29), kind=kOutput, calls=%fused_computation.38 | convolution fusion | flops 2819948544 | bytes 11730944 | tf_op jit(solution)/shard_map/dot_general | solution.py:240
  (80 shorter events, 6.5 us)
Async XLA Ops:
  6.5 61.3 %all-gather.6.cloned.1.call-start = ((), (), s32[]{:S(2)}) async-start(), calls=%async_computation.1 | async-start | bytes 2703360 | tf_op jit(solution)/shard_map/all_gather | solution.py:87
  7.3 105.1 %all-gather.4.cloned.1.call-start = ((), (), s32[]{:S(2)}) async-start(), calls=%async_computation | async-start | bytes 6881280 | tf_op jit(solution)/shard_map/all_gather | solution.py:120
  8.0 62.4 %copy-start.2 = (bf16[512,1344]{0,1:T(8,128)(2,1)S(1)}, bf16[512,1344]{0,1:T(8,128)(2,1)}, u32[]{:S(2)}) copy-start(bf16[512,1344]{0,1:T(8,128)(2,1)} %param.16) | copy-start | bytes 4128772
  8.0 237.7 %all-gather.8.cloned.1.call-start = ((), (), s32[]{:S(2)}) async-start(), calls=%async_computation.2 | async-start | bytes 2621440 | tf_op jit(solution)/shard_map/all_gather | solution.py:241
  112.4 7.7 %copy-start.7 = (bf16[512,5376]{0,1:T(8,128)(2,1)S(1)}, bf16[512,5376]{0,1:T(8,128)(2,1)}, u32[]{:S(2)}) copy-start(bf16[512,5376]{0,1:T(8,128)(2,1)} %all-gather.4.cloned.1.call-done) | copy-start | bytes 16515076
  112.4 14.5 %slice-start = ((s8[5505024]{0:T(1024)(128)(4,1)}), s8[4194304]{0:T(1024)(128)(4,1)S(1)}, s32[]{:S(2)}) async-start(s8[5505024]{0:T(1024)(128)(4,1)} %bitcast.144), calls=%async_computation.3 | async-start | bytes 8388608
  120.0 5.3 %copy-start.5 = (f32[128]{0:T(128)S(1)}, f32[128]{0:T(128)}, u32[]{:S(2)}) copy-start(f32[128]{0:T(128)} %param.22) | copy-start | bytes 1540
  120.0 5.5 %copy-start.6 = (f32[128]{0:T(128)S(1)}, f32[128]{0:T(128)}, u32[]{:S(2)}) copy-start(f32[128]{0:T(128)} %param.21) | copy-start | bytes 1540
  120.0 6.8 %slice-start.1 = ((s8[5505024]{0:T(1024)(128)(4,1)}), s8[1310720]{0:T(1024)(128)(4,1)S(1)}, s32[]{:S(2)}) async-start(s8[5505024]{0:T(1024)(128)(4,1)} %bitcast.144), calls=%async_computation.4 | async-start | bytes 2621440
  130.2 5.3 %copy-start.1 = (bf16[1,512,256]{2,1,0:T(8,128)(2,1)}, bf16[1,512,256]{2,1,0:T(8,128)(2,1)S(1)}, u32[]{:S(2)}) copy-start(bf16[1,512,256]{2,1,0:T(8,128)(2,1)S(1)} %copy.115) | copy-start | bytes 786436
  131.1 16.2 %collective-permute-start = (bf16[2,512,256]{2,1,0:T(8,128)(2,1)}, bf16[2,512,256]{2,1,0:T(8,128)(2,1)}, u32[]{:S(2)}, u32[]{:S(2)}) collective-permute-start(bf16[2,512,256]{2,1,0:T(8,128)(2,1)} %pad_maximum_fusion), channel_id=1, source_target_pairs={{0,8},{4,12},{1,9},{5,13},{2,10},{6,14},{3,11},{7,15},{16,24},{20,... | collective-permute-start | bytes 1572872 | tf_op jit(solution)/shard_map/ppermute | solution.py:20
  135.5 22.4 %collective-permute-start.1 = (bf16[2,512,256]{2,1,0:T(8,128)(2,1)}, bf16[2,512,256]{2,1,0:T(8,128)(2,1)}, u32[]{:S(2)}, u32[]{:S(2)}) collective-permute-start(bf16[2,512,256]{2,1,0:T(8,128)(2,1)} %pad_maximum_fusion), channel_id=1, source_target_pairs={{0,4},{4,8},{8,12},{1,5},{5,9},{9,13},{2,6},{6,10},{10,14},{3,7},{... | collective-permute-start | bytes 1572872 | tf_op jit(solution)/shard_map/ppermute | solution.py:20
  159.3 0.7 copy-start.4
  159.9 30.6 %copy-start.3 = (bf16[2,512,32]{1,2,0:T(8,128)(2,1)S(1)}, bf16[2,512,32]{1,2,0:T(8,128)(2,1)}, u32[]{:S(2)}) copy-start(bf16[2,512,32]{1,2,0:T(8,128)(2,1)} %param.26) | copy-start | bytes 196612
  190.5 43.5 %copy-start = (bf16[512,2,2,128]{0,3,2,1:T(8,128)(2,1)S(1)}, bf16[512,2,2,128]{0,3,2,1:T(8,128)(2,1)}, u32[]{:S(2)}) copy-start(bf16[512,2,2,128]{0,3,2,1:T(8,128)(2,1)} %divide_convert_fusion) | copy-start | bytes 1572868
Sparse Core Ops, SparseCore 0:
  8.9 58.8 all-gather.5
  69.4 42.9 all-gather.3
  190.6 33.6 all-gather.7
where the time goes:
time: 260 us
  blocking collectives  111 us (43%)
  waiting for transfers between devices  54.1 us (21%)
  matrix products  51.5 us (20%)
  between operations  13.5 us (5%)
  other arithmetic  9.9 us (4%)
  local copies, waits for them, and re-layouts  9.48 us (4%)
  starting transfers between devices  8.35 us (3%)
    all_gather x1, blocking collectives, per_device(): lax.all_gather(adapter_out_down, 'seq', axis=0, tiled=True)  26.5 us
    all_gather x1, blocking collectives, per_device(): lax.all_gather(key_value_up_panels, 'seq', axis=0, tiled=True)  23.4 us
    all_gather x1, waiting for transfers between devices, per_device(): feature_part = lax.all_gather(tokens, ('head', 'rep'), axis=1, tiled=True)  21.5 us
    all_gather x1, blocking collectives, per_device(): lax.all_gather(adapter_up_query, 'seq', axis=0, tiled=True)  16.8 us
    psum x1, blocking collectives, per_device(): lax.psum(partial_low, ('head', 'rep')).astype(jnp.bfloat16)  16.8 us
    all_gather x1, blocking collectives, per_device(): lax.all_gather(adapter_out_up, 'seq', axis=0, tiled=True)  16.2 us
    ppermute x2, waiting for transfers between devices, shifted(): return lax.ppermute(value, axis, pairs)  15.6 us
    all_gather x1, waiting for transfers between devices, per_device(): lax.all_gather(adapter_down, 'seq', axis=0, tiled=True)  15.6 us
  transfers between devices with their start and end apart: 5, of which 4 were waited for; matrix products, arithmetic and copies ran while one was open for 6% of the time, Pallas kernels for 0%

commit v1 on v0

--- a/solution.py
+++ b/solution.py
@@ -12,6 +12,7 @@
 rope_base = 10000.0
 score_scale = 168.0 ** (-0.5)
 adapter_scale = 2.0
+block_replace = lambda x_in: lax.psum(lax.psum(x_in, "rep"), "head")
 
 
 def shifted(value, axis, by):
@@ -249,7 +250,7 @@
         chosen_out_down,
         preferred_element_type=jnp.float32,
     ).reshape(tok_rows, ADAPTER_RANK)
-    output_reduced_rank = lax.psum(local_low, ("head", "rep")).astype(jnp.bfloat16)
+    output_reduced_rank = block_replace(local_low).astype(jnp.bfloat16)
     result = projected_rows + adapter_scale * jnp.einsum(
         "zch,zhp->zcp",
         output_reduced_rank.reshape(block_count, BLOCK, ADAPTER_RANK),

time: 260 us -> 277 us (1.065)
  blocking collectives: 111 us -> 122 us
  local copies, waits for them, and re-layouts: 9.48 us -> 14.8 us
    ppermute x2, waiting for transfers between devices: 15.6 us -> 0.01 us  [shifted(): return lax.ppermute(value, axis, pairs)]
    all_gather x1, blocking collectives: 26.5 us -> 40.6 us  [per_device(): lax.all_gather(adapter_out_down, 'seq', axis=0, tiled=True)]
    all_gather x1, waiting for transfers between devices: 0.02 us -> 13.8 us  [per_device(): lax.all_gather(attention_result, ('head', 'rep'), axis=1, tiled=True)]
  transfers between devices with their start and end apart: 5 -> 6, of which waited for: 4 -> 3; matrix products, arithmetic and copies ran while one was open for 6% -> 5% of each run, Pallas kernels for 0% -> 0%
where the time goes in v1:
time: 277 us; the launch traced here: 276 us
  blocking collectives  122 us (44%)
  waiting for transfers between devices  52.6 us (19%)
  matrix products  51.5 us (19%)
  local copies, waits for them, and re-layouts  14.8 us (5%)
  between operations  13.6 us (5%)
  other arithmetic  11.2 us (4%)
  starting transfers between devices  8.46 us (3%)
    all_gather x1, blocking collectives, per_device(): lax.all_gather(adapter_out_down, 'seq', axis=0, tiled=True)  40.6 us
    all_gather x1, blocking collectives, per_device(): lax.all_gather(key_value_up_panels, 'seq', axis=0, tiled=True)  23.5 us
    all_gather x1, waiting for transfers between devices, per_device(): feature_part = lax.all_gather(tokens, ('head', 'rep'), axis=1, tiled=True)  21.6 us
    all_gather x1, blocking collectives, per_device(): lax.all_gather(adapter_up_query, 'seq', axis=0, tiled=True)  16.6 us
    psum x1, blocking collectives, per_device(): lax.psum(partial_low, ('head', 'rep')).astype(jnp.bfloat16)  16.5 us
    all_gather x1, blocking collectives, per_device(): lax.all_gather(adapter_out_up, 'seq', axis=0, tiled=True)  16.1 us
    all_gather x1, waiting for transfers between devices, per_device(): lax.all_gather(adapter_down, 'seq', axis=0, tiled=True)  15.2 us
    all_gather x1, waiting for transfers between devices, per_device(): lax.all_gather(attention_result, ('head', 'rep'), axis=1, tiled=True)  13.8 us
  transfers between devices with their start and end apart: 6, of which 3 were waited for; matrix products, arithmetic and copies ran while one was open for 5% of the time, Pallas kernels for 0%

profile of v1, /device:TPU:0, one launch (start us, length us, event | category | flops | bytes accessed | tf_op | source)
XLA Modules:
  0.0 276.3 jit_solution(6094794574586651887)
XLA Ops:
  6.5 0.7 all-gather.6.cloned.1.call-update
  7.3 0.7 all-gather.4.cloned.1.call-update
  8.1 1.4 dynamic_slice.29
  9.5 16.6 %all_gather.24 = bf16[8,32,512]{2,1,0:T(8,128)(2,1)S(1)} all-gather(bf16[2,32,512]{2,1,0:T(8,128)(2,1)} %param.24), channel_id=1, replica_groups=mesh['groups'=2,'seq'=4,'head'=2,'rep'=2] {'seq'}, dimensions={0}, use_global_device_ids=true | all-gather | bytes 327680 | tf_op jit(solution)/shard_map/all_gather | solution.py:89
  26.1 0.9 convert_reduce_fusion
  27.0 0.8 fusion.62
  27.7 23.5 %all_gather.23 = bf16[8,2,32,512]{3,2,1,0:T(8,128)(2,1)S(1)} all-gather(bf16[2,2,32,512]{3,2,1,0:T(8,128)(2,1)} %param.25), channel_id=1, replica_groups=mesh['groups'=2,'seq'=4,'head'=2,'rep'=2] {'seq'}, dimensions={0}, use_global_device_ids=true | all-gather | bytes 655360 | tf_op jit(solution)/shard_map/all_gather | solution.py:90
  51.4 0.5 multiply_cosine_fusion
  52.7 15.2 %all-gather.6.cloned.1.call-done = bf16[8,1344,96]{1,2,0:T(8,128)(2,1)} async-done(((bf16[2,1344,96]{1,2,0:T(8,128)(2,1)}), bf16[8,1344,96]{1,2,0:T(8,128)(2,1)}) %all-gather.6.cloned.1.call-update) | async-done | bytes 2064400 | tf_op jit(solution)/shard_map/all_gather | solution.py:88
  67.9 2.6 convolution_convert_fusion
  71.1 16.5 %all-reduce.4 = bf16[512,96]{0,1:T(8,128)(2,1)S(1)} all-reduce(f32[512,96]{0,1:T(8,128)S(1)} %bitcast.140), channel_id=1, replica_groups=mesh['groups'=2,'seq'=4,'head'=2,'rep'=2] {'head','rep'}, use_global_device_ids=true, to_apply=%region_1.2 | all-reduce | flops 49152 | bytes 294912 | tf_op jit(solution)/shard_map/psum | solution.py:117
  88.0 1.3 copy.113
  90.7 21.6 %all-gather.4.cloned.1.call-done = bf16[512,5376]{0,1:T(8,128)(2,1)} async-done(((bf16[512,1344]{0,1:T(8,128)(2,1)}), bf16[512,5376]{0,1:T(8,128)(2,1)}) %all-gather.4.cloned.1.call-update) | async-done | bytes 5505040 | tf_op jit(solution)/shard_map/all_gather | solution.py:121
  112.3 7.6 %fusion.39 = (f32[512,4]{0,1:T(4,128)S(1)}, bf16[512,512]{0,1:T(8,128)(2,1)S(1)}) fusion(f32[512,512]{0,1:T(8,128)} %copy.113, bf16[512,5376]{0,1:T(8,128)(2,1)} %all-gather.4.cloned.1.call-done, bf16[5376,512]{1,0:T(8,128)(2,1)} %param.18), kind=kOutput, calls=%fused_computation.63 | convolution fusion | flops 2819880960 | bytes 12591104 | tf_op jit(solution)/shard_map/dot_general | solution.py:123
  120.0 5.2 %multiply_reduce_fusion = (f32[512,4]{0,1:T(4,128)S(1)}, f32[512,512]{0,1:T(8,128)S(1)}) fusion(f32[512,512]{0,1:T(8,128)S(1)} %copy.96, bf16[512,5376]{0,1:T(8,128)(2,1)S(1)} %copy-done.10, bf16[5376,512]{1,0:T(8,128)(2,1)} %param.17), kind=kOutput, calls=%fused_computation.69 | convolution fusion | flops 2819356672 | bytes 13115392 | tf_op jit(solution)/shard_map/dot_general | solution.py:122
  125.6 1.1 multiply_subtract_fusion
  126.8 3.0 %fusion.34 = bf16[512,512]{0,1:T(8,128)(2,1)S(1)} fusion(f32[512,512]{0,1:T(8,128)S(1)} %copy.91, bf16[512,5376]{0,1:T(8,128)(2,1)S(1)} %copy-done.10, bf16[5376,512]{1,0:T(8,128)(2,1)S(1)} %bitcast.145), kind=kOutput, calls=%fused_computation.56 | convolution fusion | flops 2819096576 | bytes 12582912 | tf_op jit(solution)/shard_map/dot_general | solution.py:124
  130.2 0.9 pad_maximum_fusion
  131.1 4.5 %collective-permute-start = (bf16[2,512,256]{2,1,0:T(8,128)(2,1)}, bf16[2,512,256]{2,1,0:T(8,128)(2,1)}, u32[]{:S(2)}, u32[]{:S(2)}) collective-permute-start(bf16[2,512,256]{2,1,0:T(8,128)(2,1)} %pad_maximum_fusion), channel_id=1, source_target_pairs={{0,8},{4,12},{1,9},{5,13},{2,10},{6,14},{3,11},{7,15},{16,24},{20,... | collective-permute-start | bytes 1572872 | tf_op jit(solution)/shard_map/ppermute | solution.py:21
  135.6 3.8 %collective-permute-start.1 = (bf16[2,512,256]{2,1,0:T(8,128)(2,1)}, bf16[2,512,256]{2,1,0:T(8,128)(2,1)}, u32[]{:S(2)}, u32[]{:S(2)}) collective-permute-start(bf16[2,512,256]{2,1,0:T(8,128)(2,1)} %pad_maximum_fusion), channel_id=1, source_target_pairs={{0,4},{4,8},{8,12},{1,5},{5,9},{9,13},{2,6},{6,10},{10,14},{3,7},{... | collective-permute-start | bytes 1572872 | tf_op jit(solution)/shard_map/ppermute | solution.py:21
  139.5 40.6 %all_gather.26 = bf16[8,512,32]{1,2,0:T(8,128)(2,1)S(1)} all-gather(bf16[2,512,32]{1,2,0:T(8,128)(2,1)S(1)} %copy-done.4), channel_id=1, replica_groups=mesh['groups'=2,'seq'=4,'head'=2,'rep'=2] {'seq'}, dimensions={0}, use_global_device_ids=true | all-gather | bytes 327680 | tf_op jit(solution)/shard_map/all_gather | solution.py:91
  180.7 1.4 copy.98
  182.1 1.1 fusion.41
  183.3 1.4 maximum_maximum_fusion
  185.1 0.5 iota.44
  185.7 35.2 %while.15 = (s32[]{:T(128)}, f32[512,2,2,128]{0,3,2,1:T(8,128)S(1)}, f32[2,2,512]{2,1,0:T(2,128)S(1)}, bf16[3,512,2,128]{3,2,1,0:T(2,128)(2,1)S(1)}, s32[3]{0:T(...) while((s32[]{:T(128)}, ...), condition=%wide.region_8.9_spmd.clone, body=%wide.region_5.8_spmd.clone.sunk | while | flops 543460864 | bytes 13948180 | solution.py:228
  185.7 1.2 dynamic_slice.49
  187.5 0.7 select_reduce_fusion.2
  188.3 0.7 broadcast_bitcast_fusion.2
  189.9 4.0 %fusion.93 = (f32[2,2,512]{2,1,0:T(2,128)S(1)}, f32[2,512,512,2]{2,1,3,0:T(8,128)}) fusion(pred[512,512]{0,1:T(8,128)(4,1)S(1)} %fusion.92, bf16[512,2,2,128]{3,0,2,1:T(8,128)(2,1)} %get-tuple-element.399, bf16[1,512,2,128]{3,2,1,0:T(2,128)(2,1)S(1)} %get-tuple-element.359), kind=kOutput, calls=%fused_computation.4.clone.1 | convolution fusion | flops 270530560 | bytes 5251072 | tf_op jit(solution)/shard_map/while/body/eval_jaxpr/tcpd,kcd->cptk/dot_general | solution.py:214
  194.1 3.2 %fusion.94 = f32[512,2,2,128]{0,3,2,1:T(8,128)S(1)} fusion(f32[2,512,512,2]{2,1,3,0:T(8,128)} %get-tuple-element.360, pred[512,512]{0,1:T(8,128)(4,1)S(1)} %fusion.92, f32[512,2,2,128]{0,3,2,1:T(8,128)S(1)} %get-tuple-element.378, pred[]{:T(512)S(6)} %compare.16, bf16[1,512,2,128]{1,3,2,0:T(8,128)(2,1)S(1)} %copy.178), kind=kOutput, calls=%fused_computation.12.clone.1 | convolution fusion | flops 271056896 | bytes 6815745 | tf_op jit(solution)/shard_map/while/body/eval_jaxpr/cptk,kcd->tcpd/dot_general | solution.py:220
  197.4 1.2 dynamic_slice.49
  199.3 0.7 select_reduce_fusion.2
  200.0 0.7 broadcast_bitcast_fusion.2
  201.6 4.1 %fusion.93 = (f32[2,2,512]{2,1,0:T(2,128)S(1)}, f32[2,512,512,2]{2,1,3,0:T(8,128)}) fusion(pred[512,512]{0,1:T(8,128)(4,1)S(1)} %fusion.92, bf16[512,2,2,128]{3,0,2,1:T(8,128)(2,1)} %get-tuple-element.399, bf16[1,512,2,128]{3,2,1,0:T(2,128)(2,1)S(1)} %get-tuple-element.359), kind=kOutput, calls=%fused_computation.4.clone.1 | convolution fusion | flops 270530560 | bytes 5251072 | tf_op jit(solution)/shard_map/while/body/eval_jaxpr/tcpd,kcd->cptk/dot_general | solution.py:214
  205.8 3.2 %fusion.94 = f32[512,2,2,128]{0,3,2,1:T(8,128)S(1)} fusion(f32[2,512,512,2]{2,1,3,0:T(8,128)} %get-tuple-element.360, pred[512,512]{0,1:T(8,128)(4,1)S(1)} %fusion.92, f32[512,2,2,128]{0,3,2,1:T(8,128)S(1)} %get-tuple-element.378, pred[]{:T(512)S(6)} %compare.16, bf16[1,512,2,128]{1,3,2,0:T(8,128)(2,1)S(1)} %copy.178), kind=kOutput, calls=%fused_computation.12.clone.1 | convolution fusion | flops 271056896 | bytes 6815745 | tf_op jit(solution)/shard_map/while/body/eval_jaxpr/cptk,kcd->tcpd/dot_general | solution.py:220
  209.1 1.2 dynamic_slice.49
  211.0 0.7 select_reduce_fusion.2
  211.8 0.7 broadcast_bitcast_fusion.2
  213.4 4.1 %fusion.93 = (f32[2,2,512]{2,1,0:T(2,128)S(1)}, f32[2,512,512,2]{2,1,3,0:T(8,128)}) fusion(pred[512,512]{0,1:T(8,128)(4,1)S(1)} %fusion.92, bf16[512,2,2,128]{3,0,2,1:T(8,128)(2,1)} %get-tuple-element.399, bf16[1,512,2,128]{3,2,1,0:T(2,128)(2,1)S(1)} %get-tuple-element.359), kind=kOutput, calls=%fused_computation.4.clone.1 | convolution fusion | flops 270530560 | bytes 5251072 | tf_op jit(solution)/shard_map/while/body/eval_jaxpr/tcpd,kcd->cptk/dot_general | solution.py:214
  217.6 3.2 %fusion.94 = f32[512,2,2,128]{0,3,2,1:T(8,128)S(1)} fusion(f32[2,512,512,2]{2,1,3,0:T(8,128)} %get-tuple-element.360, pred[512,512]{0,1:T(8,128)(4,1)S(1)} %fusion.92, f32[512,2,2,128]{0,3,2,1:T(8,128)S(1)} %get-tuple-element.378, pred[]{:T(512)S(6)} %compare.16, bf16[1,512,2,128]{1,3,2,0:T(8,128)(2,1)S(1)} %copy.178), kind=kOutput, calls=%fused_computation.12.clone.1 | convolution fusion | flops 271056896 | bytes 6815745 | tf_op jit(solution)/shard_map/while/body/eval_jaxpr/cptk,kcd->tcpd/dot_general | solution.py:220
  221.4 0.6 copy.174
  222.1 0.5 all-gather.8.cloned.1.call-update
  222.6 16.1 %all_gather.27 = bf16[8,32,1344]{2,1,0:T(8,128)(2,1)S(1)} all-gather(bf16[2,32,1344]{2,1,0:T(8,128)(2,1)S(1)} %copy-done.3), channel_id=1, replica_groups=mesh['groups'=2,'seq'=4,'head'=2,'rep'=2] {'seq'}, dimensions={0}, use_global_device_ids=true | all-gather | bytes 860160 | tf_op jit(solution)/shard_map/all_gather | solution.py:92
  239.2 8.8 %psum.23 = bf16[512,32]{0,1:T(8,128)(2,1)S(1)} all-reduce(f32[512,32]{0,1:T(8,128)} %all-reduce.3.cloned.1.call-done), channel_id=1, replica_groups=mesh['groups'=2,'seq'=4,'head'=2,'rep'=2] {'head'}, use_global_device_ids=true, to_apply=%region_10.11 | all-reduce | flops 16384 | bytes 98304 | tf_op jit(solution)/shard_map/psum | solution.py:15
  247.9 0.7 fusion.29
  248.6 13.8 %all-gather.8.cloned.1.call-done = bf16[512,2048]{0,1:T(8,128)(2,1)} async-done(((bf16[512,512]{0,1:T(8,128)(2,1)}), bf16[512,2048]{0,1:T(8,128)(2,1)}) %all-gather.8.cloned.1.call-update) | async-done | bytes 2097168 | tf_op jit(solution)/shard_map/all_gather | solution.py:242
  262.5 7.3 %fusion.27 = bf16[512,1344]{0,1:T(8,128)(2,1)} fusion(bf16[2048,1344]{0,1:T(8,128)(2,1)} %param.20, bf16[512,2048]{0,1:T(8,128)(2,1)} %all-gather.8.cloned.1.call-done, f32[4,168,8,128]{3,2,1,0:T(8,128)S(1)} %fusion.29), kind=kOutput, calls=%fused_computation.38 | convolution fusion | flops 2819948544 | bytes 11730944 | tf_op jit(solution)/shard_map/dot_general | solution.py:241
  (89 shorter events, 9.2 us)
Async XLA Ops:
  6.5 61.4 %all-gather.6.cloned.1.call-start = ((), (), s32[]{:S(2)}) async-start(), calls=%async_computation.1 | async-start | bytes 2703360 | tf_op jit(solution)/shard_map/all_gather | solution.py:88
  7.3 105.1 %all-gather.4.cloned.1.call-start = ((), (), s32[]{:S(2)}) async-start(), calls=%async_computation | async-start | bytes 6881280 | tf_op jit(solution)/shard_map/all_gather | solution.py:121
  8.0 62.5 %copy-start.2 = (bf16[512,1344]{0,1:T(8,128)(2,1)S(1)}, bf16[512,1344]{0,1:T(8,128)(2,1)}, u32[]{:S(2)}) copy-start(bf16[512,1344]{0,1:T(8,128)(2,1)} %param.16) | copy-start | bytes 4128772
  8.0 231.1 %all-reduce.3.cloned.1.call-start = ((), (), s32[]{:S(2)}) async-start(), calls=%async_computation.3 | async-start | bytes 131072 | tf_op jit(solution)/shard_map/psum | solution.py:15
  27.7 40.2 %copy-start.5 = (s32[4]{0:T(128)}, s32[4]{0:T(128)S(1)}, u32[]{:S(2)}) copy-start(s32[4]{0:T(128)S(1)} %fusion.62) | copy-start | bytes 52
  112.3 7.7 %copy-start.10 = (bf16[512,5376]{0,1:T(8,128)(2,1)S(1)}, bf16[512,5376]{0,1:T(8,128)(2,1)}, u32[]{:S(2)}) copy-start(bf16[512,5376]{0,1:T(8,128)(2,1)} %all-gather.4.cloned.1.call-done) | copy-start | bytes 16515076
  112.3 14.4 %slice-start = ((s8[5505024]{0:T(1024)(128)(4,1)}), s8[4194304]{0:T(1024)(128)(4,1)S(1)}, s32[]{:S(2)}) async-start(s8[5505024]{0:T(1024)(128)(4,1)} %bitcast.144), calls=%async_computation.4 | async-start | bytes 8388608
  120.0 5.3 %copy-start.8 = (f32[128]{0:T(128)S(1)}, f32[128]{0:T(128)}, u32[]{:S(2)}) copy-start(f32[128]{0:T(128)} %param.22) | copy-start | bytes 1540
  120.0 5.5 %copy-start.9 = (f32[128]{0:T(128)S(1)}, f32[128]{0:T(128)}, u32[]{:S(2)}) copy-start(f32[128]{0:T(128)} %param.21) | copy-start | bytes 1540
  120.0 6.8 %slice-start.1 = ((s8[5505024]{0:T(1024)(128)(4,1)}), s8[1310720]{0:T(1024)(128)(4,1)S(1)}, s32[]{:S(2)}) async-start(s8[5505024]{0:T(1024)(128)(4,1)} %bitcast.144), calls=%async_computation.5 | async-start | bytes 2621440
  129.8 9.7 %copy-start.4 = (bf16[2,512,32]{1,2,0:T(8,128)(2,1)S(1)}, bf16[2,512,32]{1,2,0:T(8,128)(2,1)}, u32[]{:S(2)}) copy-start(bf16[2,512,32]{1,2,0:T(8,128)(2,1)} %param.26) | copy-start | bytes 196612
  129.8 50.3 %copy-start.6 = (s32[4]{0:T(128)S(1)}, s32[4]{0:T(128)}, u32[]{:S(2)}) copy-start(s32[4]{0:T(128)} %copy-done.5) | copy-start | bytes 52
  130.2 5.5 %copy-start.1 = (bf16[1,512,256]{2,1,0:T(8,128)(2,1)}, bf16[1,512,256]{2,1,0:T(8,128)(2,1)S(1)}, u32[]{:S(2)}) copy-start(bf16[1,512,256]{2,1,0:T(8,128)(2,1)S(1)} %copy.115) | copy-start | bytes 786436
  131.1 52.1 %collective-permute-start = (bf16[2,512,256]{2,1,0:T(8,128)(2,1)}, bf16[2,512,256]{2,1,0:T(8,128)(2,1)}, u32[]{:S(2)}, u32[]{:S(2)}) collective-permute-start(bf16[2,512,256]{2,1,0:T(8,128)(2,1)} %pad_maximum_fusion), channel_id=1, source_target_pairs={{0,8},{4,12},{1,9},{5,13},{2,10},{6,14},{3,11},{7,15},{16,24},{20,... | collective-permute-start | bytes 1572872 | tf_op jit(solution)/shard_map/ppermute | solution.py:21
  135.6 47.6 %collective-permute-start.1 = (bf16[2,512,256]{2,1,0:T(8,128)(2,1)}, bf16[2,512,256]{2,1,0:T(8,128)(2,1)}, u32[]{:S(2)}, u32[]{:S(2)}) collective-permute-start(bf16[2,512,256]{2,1,0:T(8,128)(2,1)} %pad_maximum_fusion), channel_id=1, source_target_pairs={{0,4},{4,8},{8,12},{1,5},{5,9},{9,13},{2,6},{6,10},{10,14},{3,7},{... | collective-permute-start | bytes 1572872 | tf_op jit(solution)/shard_map/ppermute | solution.py:21
  220.9 1.7 copy-start.3
  220.9 17.8 %copy-start.7 = (s32[4]{0:T(128)S(1)}, s32[4]{0:T(128)}, u32[]{:S(2)}) copy-start(s32[4]{0:T(128)} %copy-done.5) | copy-start | bytes 52
  221.0 1.1 copy-start
  222.0 40.4 %all-gather.8.cloned.1.call-start = ((), (), s32[]{:S(2)}) async-start(), calls=%async_computation.2 | async-start | bytes 2621440 | tf_op jit(solution)/shard_map/all_gather | solution.py:242
Sparse Core Ops, SparseCore 0:
  8.9 58.9 all-gather.5
  69.5 42.7 all-gather.3
  222.1 15.0 all-reduce.2
  238.7 23.7 all-gather.7
